TPU v7x, 32 devices: a whole 2x2x4 slice. The times are simulated.
32 devices in a mesh: slab: 8 (over y, x, core), grp: 4 (over z).
Axes of the slice: x: 2, y: 2, z: 4, core: 2. Of those that a mesh axis runs over, the one named last changes fastest.
Arguments:
- near_field: bfloat16 [2, 4096, 2048], P(None, 'slab', 'grp'), may hold values from -6 to 6
- lens_phase: float32 [2, 4096, 2048], P(None, 'slab', 'grp'), may hold values from -3.140625 to 3.140625
Outputs:
- far_field: float32 [2, 512, 2048], P(None, ('slab', 'grp'))
All inputs are finite; a program needn't handle non-finite values.
Results may differ from a plain program's by a relative error of at most 0.0083.
Values may be sent and summed in bfloat16 or wider, within the bound.
A program may use at most 128 MiB of HBM per device.

v0:
```python
import math
import jax
import jax.numpy as jnp
from jax import lax
from jax.sharding import PartitionSpec as P

AV = 512
AL = 2048
PHASE_CODE = 40.0


def sincos(angle):
    half = 0.5 * angle
    sq = half * half
    sin = -1.0 / 39916800.0
    for term in (1.0 / 362880.0, -1.0 / 5040.0, 1.0 / 120.0, -1.0 / 6.0, 1.0):
        sin = sin * sq + term
    sin = sin * half
    cos = 1.0 / 479001600.0
    for term in (-1.0 / 3628800.0, 1.0 / 40320.0, -1.0 / 720.0, 1.0 / 24.0, -0.5, 1.0):
        cos = cos * sq + term
    return (1.0 - 2.0 * sin * sin, 2.0 * sin * cos)


def unit_angle(turns, modulus):
    assert modulus & modulus - 1 == 0
    centred = (turns + modulus // 2 & modulus - 1) - modulus // 2
    return sincos(centred.astype(jnp.float32) * (2.0 * math.pi / modulus))


def count(size):
    return lax.optimization_barrier(jnp.arange(size, dtype=jnp.int32))


def phase_table(row_index, col_index, modulus):
    cos, sin = unit_angle(row_index[:, None] * col_index[None, :], modulus)
    return (cos.astype(jnp.bfloat16), sin.astype(jnp.bfloat16))


def propagator(points):
    band = math.gcd(points, 128)
    offset = count(points)[None, :] - count(band)[:, None]
    cos, sin = unit_angle(offset * offset - points // 4, 2 * points)
    gain = 1.0 / math.sqrt(points)

    def rolled(part):
        part = lax.optimization_barrier((part * gain).astype(jnp.bfloat16))
        twice = jnp.concatenate([part, part], axis=1)
        return jnp.concatenate(
            [
                lax.slice_in_dim(twice, points - start, 2 * points - start, axis=1)
                for start in range(0, points, band)
            ]
        )

    return (rolled(cos), rolled(sin))


def matmul(left, right):
    return jnp.dot(left, right, preferred_element_type=jnp.float32)


def complex_product(both, table_cos, table_sin):
    rows = both.shape[0] // 2
    with_cos = matmul(both, table_cos)
    with_sin = matmul(both, table_sin)
    return (with_cos[:rows] - with_sin[rows:], with_sin[:rows] + with_cos[rows:])


def on_device(near_field, lens_phase):
    slab_count = lax.axis_size("slab")
    group_count = lax.axis_size("grp")
    devices = slab_count * group_count
    steps, lat_dev, width = lens_phase.shape
    points = width * group_count
    total_rows = lat_dev * slab_count
    rows = lat_dev // group_count
    angles = AV // devices
    coded = [jnp.exp2(lens_phase[k] * PHASE_CODE).astype(jnp.bfloat16) for k in range(steps)]
    field = lax.all_to_all(near_field, "grp", split_axis=1, concat_axis=2, tiled=True)
    coded = [lax.all_to_all(part, "grp", split_axis=0, concat_axis=1, tiled=True) for part in coded]
    prop_cos, prop_sin = propagator(points)
    both = field.reshape(2 * rows, points)
    for section in range(steps):
        real, imag = complex_product(both, prop_cos, prop_sin)
        real = real.astype(jnp.bfloat16).astype(jnp.float32)
        imag = imag.astype(jnp.bfloat16).astype(jnp.float32)
        phase = jnp.log2(coded[section].astype(jnp.float32)) * (1.0 / PHASE_CODE)
        lens_cos, lens_sin = sincos(phase)
        both = jnp.concatenate(
            [
                (real * lens_cos - imag * lens_sin).astype(jnp.bfloat16),
                (real * lens_sin + imag * lens_cos).astype(jnp.bfloat16),
            ]
        )
    vert_cos, vert_sin = phase_table(count(points) - points // 2, count(AV) - AV // 2, 2 * points)
    col_real, col_imag = complex_product(both, vert_cos, -vert_sin)
    cols = jnp.stack([col_real, col_imag]).astype(jnp.bfloat16)
    cols = jnp.transpose(cols.reshape(2, rows, devices, angles), (2, 0, 3, 1))
    got = lax.all_to_all(cols, ("slab", "grp"), split_axis=0, concat_axis=0, tiled=True)
    modulus = 2 * total_rows
    period = modulus // rows
    source = count(devices) - devices // 2
    fine = count(period)
    near = count(rows)
    coarse = count(AL // period)
    w_cos, w_sin = phase_table(source, fine, period)
    got_real = got[:, 0]
    got_imag = got[:, 1]
    ein = lambda s, l, r: jnp.einsum(s, l, r, preferred_element_type=jnp.float32)
    mid_real = ein("sam,sf->afm", got_real, w_cos) + ein("sam,sf->afm", got_imag, w_sin)
    mid_imag = ein("sam,sf->afm", got_imag, w_cos) - ein("sam,sf->afm", got_real, w_sin)
    t_cos, t_sin = unit_angle(fine[:, None] * near[None, :], modulus)
    turned_real = (mid_real * t_cos + mid_imag * t_sin).astype(jnp.bfloat16)
    turned_imag = (mid_imag * t_cos - mid_real * t_sin).astype(jnp.bfloat16)
    e_cos, e_sin = phase_table(near, coarse * period - AL // 2, modulus)
    out_real = ein("afm,mc->acf", turned_real, e_cos) + ein("afm,mc->acf", turned_imag, e_sin)
    out_imag = ein("afm,mc->acf", turned_imag, e_cos) - ein("afm,mc->acf", turned_real, e_sin)
    scale = 1.0 / math.sqrt(total_rows * points)
    return (jnp.stack([out_real, out_imag]) * scale).reshape(2, angles, AL)


def solution(mesh):
    return jax.shard_map(
        on_device,
        mesh=mesh,
        in_specs=(P(None, "slab", "grp"), P(None, "slab", "grp")),
        out_specs=P(None, ("slab", "grp"), None),
        check_vma=False,
    )
```

profile of v0, /device:TPU:0, one launch (start us, length us, event | category | flops | bytes accessed | tf_op | source)
XLA Modules:
  0.0 123.4 jit_solution(17463661891979874556)
XLA Ops:
  0.0 2.8 %exponential_convert_fusion.1 = (bf16[1,512,512]{2,1,0:T(8,128)(2,1)}, bf16[1,512,512]{2,1,0:T(8,128)(2,1)}) fusion(f32[2,512,512]{2,1,0:T(8,128)} %param.3), kind=kLoop, calls=%fused_computation.138 | loop fusion | flops 1048576 | bytes 3145728 | tf_op jit(solution)/shard_map/convert_element_type | solution.py:79
  2.8 6.3 %all-to-all-start.1 = ((bf16[4,128,512]{2,1,0:T(8,128)(2,1)}), bf16[4,128,512]{2,1,0:T(8,128)(2,1)S(1)}, u32[]{:S(2)}, u32[]{:S(2)}) async-start(bf16[4,128,512]{2,1,0:T(8,128)(2,1)} %bitcast.6), calls=%async_computation.1 | async-start | bytes 1048576 | tf_op jit(solution)/shard_map/all_to_all | solution.py:81
  9.2 1.4 %fusion.27 = (bf16[128,2048]{1,0:T(8,128)(2,1)S(1)}, bf16[128,2048]{1,0:T(8,128)(2,1)S(1)}) fusion(s32[128]{0:T(128)S(1)} %iota.18, s32[2048]{0:T(1024)S(1)} %iota.21), kind=kLoop, calls=%fused_computation.108 | loop fusion | flops 10223616 | bytes 1057280 | tf_op jit(solution)/shard_map/convert_element_type | solution.py:47
  11.3 0.9 constant_dynamic-update-slice_fusion
  12.2 1.3 %fusion.76 = bf16[2048,2048]{1,0:T(8,128)(2,1)} fusion(bf16[2048,2048]{1,0:T(8,128)(2,1)} %constant_dynamic-update-slice_fusion, bf16[128,2048]{1,0:T(8,128)(2,1)S(1)} %get-tuple-element.20), kind=kLoop, calls=%fused_computation.180 | loop fusion | flops 1048576 | bytes 1048576
  13.6 0.8 fusion.78
  14.4 0.9 fusion.80
  15.3 0.8 fusion.82
  16.1 0.8 fusion.84
  16.9 0.8 fusion.86
  17.8 0.9 fusion.88
  18.6 0.9 fusion.90
  19.5 4.1 %all-to-all-done.1 = bf16[4,128,512]{2,1,0:T(8,128)(2,1)S(1)} async-done(((bf16[4,128,512]{2,1,0:T(8,128)(2,1)}), bf16[4,128,512]{2,1,0:T(8,128)(2,1)S(1)}, u32[]{:S(2)}, u32[]{:S(2)}) %all-to-all-start.1) | async-done | bytes 524320 | tf_op jit(solution)/shard_map/all_to_all | solution.py:81
  23.6 3.5 %all-to-all-start.2 = ((bf16[4,128,512]{2,1,0:T(8,128)(2,1)}), bf16[4,128,512]{2,1,0:T(8,128)(2,1)S(1)}, u32[]{:S(2)}, u32[]{:S(2)}) async-start(bf16[4,128,512]{2,1,0:T(8,128)(2,1)} %bitcast.8), calls=%async_computation.2 | async-start | bytes 1048576 | tf_op jit(solution)/shard_map/all_to_all | solution.py:81
  27.1 2.1 %copy.14 = bf16[2,512,512]{2,0,1:T(2,128)(2,1)} copy(bf16[2,512,512]{2,1,0:T(8,128)(2,1)S(1)} %copy-done.1) | data formatting | bytes 2097152 | tf_op args[0]
  29.2 0.8 fusion.92
  30.1 0.9 fusion.94
  30.9 0.9 fusion.96
  31.8 9.4 %all-to-all-done.2 = bf16[4,128,512]{2,1,0:T(8,128)(2,1)S(1)} async-done(((bf16[4,128,512]{2,1,0:T(8,128)(2,1)}), bf16[4,128,512]{2,1,0:T(8,128)(2,1)S(1)}, u32[]{:S(2)}, u32[]{:S(2)}) %all-to-all-start.2) | async-done | bytes 524320 | tf_op jit(solution)/shard_map/all_to_all | solution.py:81
  41.1 3.7 %all-to-all-start = ((bf16[2,512,512]{2,0,1:T(2,128)(2,1)}), bf16[2,512,512]{2,0,1:T(2,128)(2,1)S(1)}, u32[]{:S(2)}, u32[]{:S(2)}) async-start(bf16[2,512,512]{2,0,1:T(2,128)(2,1)} %copy.14), calls=%async_computation | async-start | bytes 2097152 | tf_op jit(solution)/shard_map/all_to_all | solution.py:80
  44.9 0.8 fusion.98
  45.7 0.8 fusion.100
  46.5 0.8 fusion.74
  47.4 0.8 fusion.102
  48.5 1.2 multiply_bitcast_fusion
  49.8 20.1 %all-to-all-done = bf16[2,512,512]{2,0,1:T(2,128)(2,1)S(1)} async-done(((bf16[2,512,512]{2,0,1:T(2,128)(2,1)}), bf16[2,512,512]{2,0,1:T(2,128)(2,1)S(1)}, u32[]{:S(2)}, u32[]{:S(2)}) %all-to-all-start) | async-done | bytes 1048608 | tf_op jit(solution)/shard_map/all_to_all | solution.py:80
  69.9 0.8 copy.15
  71.0 5.9 %convolution_bitcast_fusion = f32[256,2048]{1,0:T(8,128)S(1)} fusion(bf16[256,2048]{1,0:T(8,128)(2,1)S(1)} %bitcast.77, bf16[2048,2048]{1,0:T(8,128)(2,1)} %copy-done.2), kind=kOutput, calls=%fused_computation.69 | convolution fusion | flops 2147483648 | bytes 11534336 | tf_op jit(solution)/shard_map/dot_general | solution.py:60
  76.9 5.9 %convolution_bitcast_fusion.1 = f32[256,2048]{1,0:T(8,128)S(1)} fusion(bf16[256,2048]{1,0:T(8,128)(2,1)S(1)} %bitcast.78, bf16[2048,2048]{1,0:T(8,128)(2,1)} %fusion.102), kind=kOutput, calls=%fused_computation.70 | convolution fusion | flops 2147483648 | bytes 11534336 | tf_op jit(solution)/shard_map/dot_general | solution.py:60
  82.8 1.2 fusion.16
  84.0 1.1 fusion.18
  85.2 2.4 %fusion.43 = f32[256,2048]{1,0:T(8,128)S(1)} fusion(bf16[2048,2048]{1,0:T(8,128)(2,1)S(1)} %bitcast.82, bf16[128,2048]{1,0:T(8,128)(2,1)S(1)} %fusion.18, bf16[128,2048]{1,0:T(8,128)(2,1)S(1)} %get-tuple-element.8), kind=kOutput, calls=%fused_computation.147 | convolution fusion | flops 2149580800 | bytes 11534336 | tf_op jit(solution)/shard_map/dot_general | solution.py:60
  87.6 5.7 %fusion.44 = f32[256,2048]{1,0:T(8,128)S(1)} fusion(bf16[2048,2048]{1,0:T(8,128)(2,1)} %fusion.102, bf16[128,2048]{1,0:T(8,128)(2,1)S(1)} %fusion.18, bf16[128,2048]{1,0:T(8,128)(2,1)S(1)} %get-tuple-element.8), kind=kOutput, calls=%fused_computation.148 | convolution fusion | flops 2149580800 | bytes 11534336 | tf_op jit(solution)/shard_map/dot_general | solution.py:60
  93.3 1.4 %fusion.20 = (bf16[128,2048]{1,0:T(8,128)(2,1)S(1)}, bf16[128,2048]{1,0:T(8,128)(2,1)S(1)}, bf16[128,2048]{1,0:T(8,128)(2,1)S(1)}) fusion(f32[128,2048]{1,0:T(8,128)S(1)} %bitcast.71, f32[256,2048]{1,0:T(8,128)S(1)} %fusion.44, f32[256,2048]{1,0:T(8,128)S(1)} %fusion.43), kind=kLoop, calls=%fused_computation.101 | loop fusion | flops 9961472 | bytes 6815744 | tf_op jit(solution)/shard_map/convert_element_type | solution.py:92
  94.7 1.1 fusion.22
  95.9 3.4 %fusion.6 = f32[256,512]{1,0:T(8,128)S(1)} fusion(s32[512]{0:T(512)S(1)} %broadcast_add_fusion.1, s32[2048]{0:T(1024)S(1)} %broadcast_add_fusion, bf16[128,2048]{1,0:T(8,128)(2,1)S(1)} %fusion.22, bf16[128,2048]{1,0:T(8,128)(2,1)S(1)} %get-tuple-element.5), kind=kOutput, calls=%fused_computation.71 | convolution fusion | flops 562036736 | bytes 1583104 | tf_op jit(solution)/shard_map/dot_general | solution.py:60
  99.3 5.0 %fusion.8 = f32[256,512]{1,0:T(8,128)S(1)} fusion(s32[512]{0:T(512)S(1)} %broadcast_add_fusion.1, s32[2048]{0:T(1024)S(1)} %broadcast_add_fusion, bf16[128,2048]{1,0:T(8,128)(2,1)S(1)} %fusion.22, bf16[128,2048]{1,0:T(8,128)(2,1)S(1)} %get-tuple-element.5), kind=kOutput, calls=%fused_computation.72 | convolution fusion | flops 576716800 | bytes 1583104 | tf_op jit(solution)/shard_map/dot_general | solution.py:60
  104.7 0.7 copy.20
  105.5 3.7 %all-to-all-start.3 = ((bf16[32,2,16,128]{3,2,1,0:T(8,128)(2,1)}), bf16[32,2,16,128]{3,2,1,0:T(8,128)(2,1)S(1)}, u32[]{:S(2)}, u32[]{:S(2)}) async-start(bf16[32,2,16,128]{3,2,1,0:T(8,128)(2,1)} %copy.20), calls=%async_computation.3 | async-start | bytes 524288 | tf_op jit(solution)/shard_map/all_to_all | solution.py:100
  109.3 10.1 %all-to-all-done.3 = bf16[32,2,16,128]{3,2,1,0:T(8,128)(2,1)S(1)} async-done(((bf16[32,2,16,128]{3,2,1,0:T(8,128)(2,1)}), bf16[32,2,16,128]{3,2,1,0:T(8,128)(2,1)S(1)}, u32[]{:S(2)}, u32[]{:S(2)}) %all-to-all-start.3) | async-done | bytes 262176 | tf_op jit(solution)/shard_map/all_to_all | solution.py:100
  119.4 0.3 fusion.108
  120.1 0.3 convolution_subtract_fusion
  120.5 0.4 fusion.103
  120.9 0.4 fusion.137
  121.3 0.4 fusion.135
  121.7 0.4 fusion.14
  122.2 0.4 fusion.13
  122.7 0.7 maximum_multiply_fusion
  (48 shorter events, 2.4 us)
Async XLA Ops:
  2.8 20.8 %all-to-all-start.1 = ((bf16[4,128,512]{2,1,0:T(8,128)(2,1)}), bf16[4,128,512]{2,1,0:T(8,128)(2,1)S(1)}, u32[]{:S(2)}, u32[]{:S(2)}) async-start(bf16[4,128,512]{2,1,0:T(8,128)(2,1)} %bitcast.6), calls=%async_computation.1 | async-start | bytes 1048576 | tf_op jit(solution)/shard_map/all_to_all | solution.py:81
  11.3 7.3 %copy-start.2 = (bf16[2048,2048]{1,0:T(8,128)(2,1)}, bf16[2048,2048]{1,0:T(8,128)(2,1)S(1)}, u32[]{:S(2)}) copy-start(bf16[2048,2048]{1,0:T(8,128)(2,1)S(1)} %fusion.101) | copy-start | bytes 25165828
  13.6 13.6 %copy-start.1 = (bf16[2,512,512]{2,1,0:T(8,128)(2,1)S(1)}, bf16[2,512,512]{2,1,0:T(8,128)(2,1)}, u32[]{:S(2)}) copy-start(bf16[2,512,512]{2,1,0:T(8,128)(2,1)} %param.2) | copy-start | bytes 3145732
  23.6 17.5 %all-to-all-start.2 = ((bf16[4,128,512]{2,1,0:T(8,128)(2,1)}), bf16[4,128,512]{2,1,0:T(8,128)(2,1)S(1)}, u32[]{:S(2)}, u32[]{:S(2)}) async-start(bf16[4,128,512]{2,1,0:T(8,128)(2,1)} %bitcast.8), calls=%async_computation.2 | async-start | bytes 1048576 | tf_op jit(solution)/shard_map/all_to_all | solution.py:81
  41.1 7.1 %copy-start = (bf16[4,128,512]{2,1,0:T(8,128)(2,1)}, bf16[4,128,512]{2,1,0:T(8,128)(2,1)S(1)}, u32[]{:S(2)}) copy-start(bf16[4,128,512]{2,1,0:T(8,128)(2,1)S(1)} %all-to-all-done.2) | copy-start | bytes 1572868
  41.1 28.8 %all-to-all-start = ((bf16[2,512,512]{2,0,1:T(2,128)(2,1)}), bf16[2,512,512]{2,0,1:T(2,128)(2,1)S(1)}, u32[]{:S(2)}, u32[]{:S(2)}) async-start(bf16[2,512,512]{2,0,1:T(2,128)(2,1)} %copy.14), calls=%async_computation | async-start | bytes 2097152 | tf_op jit(solution)/shard_map/all_to_all | solution.py:80
  71.0 14.2 %slice-start = ((s8[8388608]{0:T(1024)(128)(4,1)}), s8[4194304]{0:T(1024)(128)(4,1)S(1)}, s32[]{:S(2)}) async-start(s8[8388608]{0:T(1024)(128)(4,1)} %bitcast.81), calls=%async_computation.4 | async-start | bytes 8388608
  76.9 8.3 %slice-start.1 = ((s8[8388608]{0:T(1024)(128)(4,1)}), s8[4194304]{0:T(1024)(128)(4,1)S(1)}, s32[]{:S(2)}) async-start(s8[8388608]{0:T(1024)(128)(4,1)} %bitcast.81), calls=%async_computation.5 | async-start | bytes 8388608
  105.5 13.9 %all-to-all-start.3 = ((bf16[32,2,16,128]{3,2,1,0:T(8,128)(2,1)}), bf16[32,2,16,128]{3,2,1,0:T(8,128)(2,1)S(1)}, u32[]{:S(2)}, u32[]{:S(2)}) async-start(bf16[32,2,16,128]{3,2,1,0:T(8,128)(2,1)} %copy.20), calls=%async_computation.3 | async-start | bytes 524288 | tf_op jit(solution)/shard_map/all_to_all | solution.py:100
where the time goes:
time: 124 us; the launch traced here: 123 us
  waiting for transfers between devices  43.7 us (35%)
  matrix products  31.3 us (25%)
  other arithmetic  25.2 us (20%)
  starting transfers between devices  17.2 us (14%)
  local copies, waits for them, and re-layouts  5.58 us (4%)
    dot_general x6, matrix products, matmul(): return jnp.dot(left, right, preferred_element_type=jnp.float32)  28.3 us
    all_to_all x1, waiting for transfers between devices, on_device(): lax.all_to_all(near_field, 'grp', split_axis=1, concat_axis=2, tiled=True)  20.1 us
    unnamed x31, other arithmetic  14.3 us
    all_to_all x2, waiting for transfers between devices, on_device(): lax.all_to_all(part, 'grp', split_axis=0, concat_axis=1, tiled=True)  13.5 us
    all_to_all x1, waiting for transfers between devices, on_device(): lax.all_to_all(cols, ('slab', 'grp'), split_axis=0, concat_axis=0, tiled=...  10.1 us
    all_to_all x2, starting transfers between devices, on_device(): lax.all_to_all(part, 'grp', split_axis=0, concat_axis=1, tiled=True)  9.82 us
    all_to_all x1, starting transfers between devices, on_device(): lax.all_to_all(cols, ('slab', 'grp'), split_axis=0, concat_axis=0, tiled=...  3.71 us
    all_to_all x1, starting transfers between devices, on_device(): lax.all_to_all(near_field, 'grp', split_axis=1, concat_axis=2, tiled=True)  3.7 us
  transfers between devices with their start and end apart: 4, of which 4 were waited for; matrix products, arithmetic and copies ran while one was open for 16% of the time, Pallas kernels for 0%

commit v1 on v0

--- a/solution.py
+++ b/solution.py
@@ -7,6 +7,38 @@
 AV = 512
 AL = 2048
 PHASE_CODE = 40.0
+
+
+def raise_lots_all(block_here, which_dim, q_in):
+    v_now = block_here.shape
+    w2 = jnp.moveaxis(
+        block_here.reshape(
+            *v_now[:which_dim], q_in, v_now[which_dim] // q_in, *v_now[which_dim + 1 :]
+        ),
+        which_dim,
+        0,
+    )
+    return w2
+
+
+def deliver_edges_on_mesh(u_in, in_dim):
+    local_out = list(u_in.shape[1:])
+    local_out[in_dim] *= u_in.shape[0]
+    r2 = jnp.moveaxis(u_in, 0, in_dim).reshape(local_out)
+    return r2
+
+
+def members_all_form(a0, net_axis, inp, in_array=2):
+    o_now, new = (lax.axis_size(net_axis), lax.axis_index(net_axis))
+    base_arr = raise_lots_all(a0, inp, o_now)
+    parts_seen = [base_arr[new]]
+    for m in [*range(1, o_now)]:
+        outcome_arr = base_arr[new ^ m]
+        value_now = lax.ppermute(outcome_arr, net_axis, [(at, at ^ m) for at in range(o_now)])
+        parts_seen.append(value_now)
+    base_arr = jnp.stack(parts_seen, 0)[new ^ jnp.arange(o_now)]
+    oldest = deliver_edges_on_mesh(base_arr, in_array)
+    return oldest
 
 
 def sincos(angle):
@@ -77,7 +109,7 @@
     rows = lat_dev // group_count
     angles = AV // devices
     coded = [jnp.exp2(lens_phase[k] * PHASE_CODE).astype(jnp.bfloat16) for k in range(steps)]
-    field = lax.all_to_all(near_field, "grp", split_axis=1, concat_axis=2, tiled=True)
+    field = members_all_form(near_field, "grp", 1)
     coded = [lax.all_to_all(part, "grp", split_axis=0, concat_axis=1, tiled=True) for part in coded]
     prop_cos, prop_sin = propagator(points)
     both = field.reshape(2 * rows, points)

time: 124 us -> 99.5 us (0.80)
  waiting for transfers between devices: 43.7 us -> 19.1 us
  other arithmetic: 25.2 us -> 11.5 us
  starting transfers between devices: 17.2 us -> 27 us
  local copies, waits for them, and re-layouts: 5.58 us -> 10 us
    all_to_all x1 -> x0, waiting for transfers between devices: 20.1 us -> none  [on_device(): lax.all_to_all(near_field, 'grp', split_axis=1, concat_axis=2, tiled=True)]
    unnamed x31 -> x32, other arithmetic: 14.3 us -> 1.38 us
    all_to_all x2, waiting for transfers between devices: 13.5 us -> 1.11 us  [on_device(): lax.all_to_all(part, 'grp', split_axis=0, concat_axis=1, tiled=True)]
    ppermute x0 -> x3, waiting for transfers between devices: none -> 7.89 us  [members_all_form(): lax.ppermute(outcome_arr, net_axis, [(at, at ^ m) for at in range(o_now)])]
    ppermute x0 -> x3, starting transfers between devices: none -> 5.71 us  [members_all_form(): lax.ppermute(outcome_arr, net_axis, [(at, at ^ m) for at in range(o_now)])]
    all_to_all x2, starting transfers between devices: 9.82 us -> 15.2 us  [on_device(): lax.all_to_all(part, 'grp', split_axis=0, concat_axis=1, tiled=True)]
    all_to_all x1 -> x0, starting transfers between devices: 3.7 us -> none  [on_device(): lax.all_to_all(near_field, 'grp', split_axis=1, concat_axis=2, tiled=True)]
    unnamed x14 -> x19, local copies, waits for them, and re-layouts: 3.35 us -> 5.86 us
  transfers between devices with their start and end apart: 4 -> 6, of which waited for: 4 -> 3; matrix products, arithmetic and copies ran while one was open for 16% -> 30% of each run, Pallas kernels for 0% -> 0%
where the time goes in v1:
time: 99.5 us; the launch traced here: 99.1 us
  matrix products  30.9 us (31%)
  starting transfers between devices  27 us (27%)
  waiting for transfers between devices  19.1 us (19%)
  other arithmetic  11.5 us (12%)
  local copies, waits for them, and re-layouts  10 us (10%)
    dot_general x6, matrix products, matmul(): return jnp.dot(left, right, preferred_element_type=jnp.float32)  28 us
    all_to_all x2, starting transfers between devices, on_device(): lax.all_to_all(part, 'grp', split_axis=0, concat_axis=1, tiled=True)  15.2 us
    all_to_all x1, waiting for transfers between devices, on_device(): lax.all_to_all(cols, ('slab', 'grp'), split_axis=0, concat_axis=0, tiled=...  10.1 us
    ppermute x3, waiting for transfers between devices, members_all_form(): lax.ppermute(outcome_arr, net_axis, [(at, at ^ m) for at in range(o_now)])  7.89 us
    all_to_all x1, starting transfers between devices, on_device(): lax.all_to_all(cols, ('slab', 'grp'), split_axis=0, concat_axis=0, tiled=...  6.07 us
    unnamed x19, local copies, waits for them, and re-layouts  5.86 us
    ppermute x3, starting transfers between devices, members_all_form(): lax.ppermute(outcome_arr, net_axis, [(at, at ^ m) for at in range(o_now)])  5.71 us
    dot_general x8, matrix products, on_device(): jnp.einsum(s, l, r, preferred_element_type=jnp.float32)  2.95 us
  transfers between devices with their start and end apart: 6, of which 3 were waited for; matrix products, arithmetic and copies ran while one was open for 30% of the time, Pallas kernels for 0%

profile of v1, /device:TPU:0, one launch (start us, length us, event | category | flops | bytes accessed | tf_op | source)
XLA Modules:
  0.0 99.1 jit_solution(3800332659667220720)
XLA Ops:
  0.0 1.3 %dynamic-slice_bitcast_fusion.3 = (bf16[1,2,128,512]{3,2,1,0:T(8,128)(2,1)S(1)}, bf16[2,128,512]{2,1,0:T(8,128)(2,1)S(1)}, bf16[2,128,512]{2,1,0:T(8,128)(2,1)S(1)}, bf16[2,128,512]{2,1,0:T(8,128)(2,1)S(1)}) fusion(bf16[2,4,128,512]{3,2,1,0:T(8,128)(2,1)} %bitcast.95, s32[]{:T(128)S(6)} %select_n.22, s32[]{:T(128)S(6)} %select_n.24, s32[]{:T(128)S(6)} %select_n.23, ...), kind=kLoop, calls=%fused_computation.222 | loop fusion | bytes 2097168 | tf_op jit(solution)/shard_map/dynamic_slice | solution.py:34
  1.3 3.1 %collective-permute-start = (bf16[2,128,512]{2,1,0:T(8,128)(2,1)S(1)}, bf16[2,128,512]{2,1,0:T(8,128)(2,1)S(1)}, u32[]{:S(2)}, u32[]{:S(2)}) collective-permute-start(bf16[2,128,512]{2,1,0:T(8,128)(2,1)S(1)} %get-tuple-element.19), channel_id=1, source_target_pairs={{0,1},{1,0},{2,3},{3,2},{4,5},{5,4},{6,7},{7,6},{8,9},{9,8},{10,11... | collective-permute-start | bytes 786440 | tf_op jit(solution)/shard_map/ppermute | solution.py:37
  4.4 2.6 %collective-permute-start.1 = (bf16[2,128,512]{2,1,0:T(8,128)(2,1)S(1)}, bf16[2,128,512]{2,1,0:T(8,128)(2,1)S(1)}, u32[]{:S(2)}, u32[]{:S(2)}) collective-permute-start(bf16[2,128,512]{2,1,0:T(8,128)(2,1)S(1)} %get-tuple-element.18), channel_id=1, source_target_pairs={{0,2},{1,3},{2,0},{3,1},{4,6},{5,7},{6,4},{7,5},{8,10},{9,11},{10,... | collective-permute-start | bytes 786440 | tf_op jit(solution)/shard_map/ppermute | solution.py:37
  7.0 2.8 %exponential_convert_fusion.1 = (bf16[1,512,512]{2,1,0:T(8,128)(2,1)}, bf16[1,512,512]{2,1,0:T(8,128)(2,1)}) fusion(f32[2,512,512]{2,1,0:T(8,128)} %param.3), kind=kLoop, calls=%fused_computation.138 | loop fusion | flops 1048576 | bytes 3145728 | tf_op jit(solution)/shard_map/convert_element_type | solution.py:111
  9.8 5.1 %all-to-all-start = ((bf16[4,128,512]{2,1,0:T(8,128)(2,1)}), bf16[4,128,512]{2,1,0:T(8,128)(2,1)S(1)}, u32[]{:S(2)}, u32[]{:S(2)}) async-start(bf16[4,128,512]{2,1,0:T(8,128)(2,1)} %bitcast.12), calls=%async_computation | async-start | bytes 1048576 | tf_op jit(solution)/shard_map/all_to_all | solution.py:113
  15.0 1.4 %fusion.27 = (bf16[128,2048]{1,0:T(8,128)(2,1)S(1)}, bf16[128,2048]{1,0:T(8,128)(2,1)S(1)}) fusion(s32[128]{0:T(128)S(1)} %iota.22, s32[2048]{0:T(1024)S(1)} %iota.26), kind=kLoop, calls=%fused_computation.107 | loop fusion | flops 10223616 | bytes 1057280 | tf_op jit(solution)/shard_map/convert_element_type | solution.py:79
  17.5 2.8 %copy-done.2 = bf16[2048,2048]{1,0:T(8,128)(2,1)} copy-done((bf16[2048,2048]{1,0:T(8,128)(2,1)}, bf16[2048,2048]{1,0:T(8,128)(2,1)S(1)}, u32[]{:S(2)}) %copy-start.2) | copy-done | bytes 8388632
  20.7 7.9 %collective-permute-done.1 = bf16[2,128,512]{2,1,0:T(8,128)(2,1)S(1)} collective-permute-done((bf16[2,128,512]{2,1,0:T(8,128)(2,1)S(1)}, bf16[2,128,512]{2,1,0:T(8,128)(2,1)S(1)}, u32[]{:S(2)}, u32[]{:S(2)}) %collective-permute-start.1) | collective-permute-done | bytes 262176 | tf_op jit(solution)/shard_map/ppermute | solution.py:37
  28.6 0.1 pad_maximum_fusion
  28.7 0.6 gather_fusion
  29.3 0.8 copy.28
  30.2 0.3 copy.44
  30.5 5.9 %fusion.294 = f32[256,2048]{1,0:T(8,128)S(1)} fusion(bf16[256,2048]{1,0:T(8,128)(2,1)S(1)} %bitcast.96, bf16[2048,2048]{1,0:T(8,128)(2,1)} %copy-done.2), kind=kOutput, calls=%fused_computation.427 | convolution fusion | flops 2147483648 | bytes 11534336 | tf_op jit(solution)/shard_map/dot_general | solution.py:92
  36.4 3.8 %fusion.293 = f32[256,2048]{1,0:T(8,128)} fusion(bf16[256,2048]{1,0:T(8,128)(2,1)S(1)} %bitcast.97, bf16[2048,2048]{1,0:T(8,128)(2,1)S(1)} %bitcast.104), kind=kOutput, calls=%fused_computation.426 | convolution fusion | flops 2147483648 | bytes 11534336 | tf_op jit(solution)/shard_map/dot_general | solution.py:92
  40.2 1.1 %all-to-all-done = bf16[4,128,512]{2,1,0:T(8,128)(2,1)S(1)} async-done(((bf16[4,128,512]{2,1,0:T(8,128)(2,1)}), bf16[4,128,512]{2,1,0:T(8,128)(2,1)S(1)}, u32[]{:S(2)}, u32[]{:S(2)}) %all-to-all-start) | async-done | bytes 524320 | tf_op jit(solution)/shard_map/all_to_all | solution.py:113
  41.3 10.2 %all-to-all-start.1 = ((bf16[4,128,512]{2,1,0:T(8,128)(2,1)}), bf16[4,128,512]{2,1,0:T(8,128)(2,1)S(1)}, u32[]{:S(2)}, u32[]{:S(2)}) async-start(bf16[4,128,512]{2,1,0:T(8,128)(2,1)} %bitcast.94), calls=%async_computation.1 | async-start | bytes 1048576 | tf_op jit(solution)/shard_map/all_to_all | solution.py:113
  51.4 0.2 multiply_bitcast_fusion.1
  51.6 0.1 copy.42
  51.7 1.3 %copy-done = f32[256,2048]{1,0:T(8,128)S(1)} copy-done((f32[256,2048]{1,0:T(8,128)S(1)}, f32[256,2048]{1,0:T(8,128)}, u32[]{:S(2)}) %copy-start) | copy-done | bytes 2097176
  53.0 1.2 %fusion.16 = (bf16[128,2048]{1,0:T(8,128)(2,1)S(1)}, bf16[128,2048]{1,0:T(8,128)(2,1)S(1)}, bf16[128,2048]{1,0:T(8,128)(2,1)S(1)}) fusion(f32[128,2048]{1,0:T(8,128)S(1)} %bitcast.88, f32[256,2048]{1,0:T(8,128)S(1)} %copy-done, f32[256,2048]{1,0:T(8,128)S(1)} %fusion.294), kind=kLoop, calls=%fused_computation.96 | loop fusion | flops 9961472 | bytes 6815744 | tf_op jit(solution)/shard_map/convert_element_type | solution.py:124
  54.2 1.1 %fusion.18 = bf16[128,2048]{1,0:T(8,128)(2,1)S(1)} fusion(bf16[128,2048]{1,0:T(8,128)(2,1)S(1)} %get-tuple-element.10, bf16[128,2048]{1,0:T(8,128)(2,1)S(1)} %get-tuple-element.9, f32[128,2048]{1,0:T(8,128)S(1)} %bitcast.89), kind=kLoop, calls=%fused_computation.98 | loop fusion | flops 8912896 | bytes 2621440 | tf_op jit(solution)/shard_map/convert_element_type | solution.py:125
  55.4 5.9 %fusion.43 = f32[256,2048]{1,0:T(8,128)S(1)} fusion(bf16[2048,2048]{1,0:T(8,128)(2,1)} %copy-done.2, bf16[128,2048]{1,0:T(8,128)(2,1)S(1)} %fusion.18, bf16[128,2048]{1,0:T(8,128)(2,1)S(1)} %get-tuple-element.8), kind=kOutput, calls=%fused_computation.147 | convolution fusion | flops 2149580800 | bytes 11534336 | tf_op jit(solution)/shard_map/dot_general | solution.py:92
  61.3 3.8 %fusion.44 = f32[256,2048]{1,0:T(8,128)} fusion(bf16[2048,2048]{1,0:T(8,128)(2,1)S(1)} %bitcast.106, bf16[128,2048]{1,0:T(8,128)(2,1)S(1)} %fusion.18, bf16[128,2048]{1,0:T(8,128)(2,1)S(1)} %get-tuple-element.8), kind=kOutput, calls=%fused_computation.148 | convolution fusion | flops 2149580800 | bytes 11534336 | tf_op jit(solution)/shard_map/dot_general | solution.py:92
  65.1 0.2 multiply_bitcast_fusion
  65.2 0.1 copy.43
  65.3 1.3 %copy-done.1 = f32[256,2048]{1,0:T(8,128)S(1)} copy-done((f32[256,2048]{1,0:T(8,128)S(1)}, f32[256,2048]{1,0:T(8,128)}, u32[]{:S(2)}) %copy-start.1) | copy-done | bytes 2097176
  66.7 1.2 %fusion.20 = (bf16[128,2048]{1,0:T(8,128)(2,1)S(1)}, bf16[128,2048]{1,0:T(8,128)(2,1)S(1)}, bf16[128,2048]{1,0:T(8,128)(2,1)S(1)}) fusion(f32[128,2048]{1,0:T(8,128)S(1)} %bitcast.90, f32[256,2048]{1,0:T(8,128)S(1)} %copy-done.1, f32[256,2048]{1,0:T(8,128)S(1)} %fusion.43), kind=kLoop, calls=%fused_computation.100 | loop fusion | flops 9961472 | bytes 6815744 | tf_op jit(solution)/shard_map/convert_element_type | solution.py:124
  67.9 1.1 %fusion.22 = bf16[128,2048]{1,0:T(8,128)(2,1)S(1)} fusion(bf16[128,2048]{1,0:T(8,128)(2,1)S(1)} %get-tuple-element.7, bf16[128,2048]{1,0:T(8,128)(2,1)S(1)} %get-tuple-element.6, f32[128,2048]{1,0:T(8,128)S(1)} %bitcast.91), kind=kLoop, calls=%fused_computation.102 | loop fusion | flops 8912896 | bytes 2621440 | tf_op jit(solution)/shard_map/convert_element_type | solution.py:125
  69.0 3.6 %fusion.6 = f32[256,512]{1,0:T(8,128)S(1)} fusion(s32[512]{0:T(512)S(1)} %broadcast_add_fusion.1, s32[2048]{0:T(1024)S(1)} %broadcast_add_fusion, bf16[128,2048]{1,0:T(8,128)(2,1)S(1)} %fusion.22, bf16[128,2048]{1,0:T(8,128)(2,1)S(1)} %get-tuple-element.5), kind=kOutput, calls=%fused_computation.70 | convolution fusion | flops 562036736 | bytes 1583104 | tf_op jit(solution)/shard_map/dot_general | solution.py:92
  72.6 5.0 %fusion.8 = f32[256,512]{1,0:T(8,128)S(1)} fusion(s32[512]{0:T(512)S(1)} %broadcast_add_fusion.1, s32[2048]{0:T(1024)S(1)} %broadcast_add_fusion, bf16[128,2048]{1,0:T(8,128)(2,1)S(1)} %fusion.22, bf16[128,2048]{1,0:T(8,128)(2,1)S(1)} %get-tuple-element.5), kind=kOutput, calls=%fused_computation.71 | convolution fusion | flops 576716800 | bytes 1583104 | tf_op jit(solution)/shard_map/dot_general | solution.py:92
  77.7 0.1 fusion.106
  77.8 0.1 copy.31
  77.9 0.1 copy.32
  78.1 0.7 copy.33
  78.8 6.1 %all-to-all-start.2 = ((bf16[32,2,16,128]{3,2,1,0:T(8,128)(2,1)}), bf16[32,2,16,128]{3,2,1,0:T(8,128)(2,1)S(1)}, u32[]{:S(2)}, u32[]{:S(2)}) async-start(bf16[32,2,16,128]{3,2,1,0:T(8,128)(2,1)} %copy.33), calls=%async_computation.2 | async-start | bytes 524288 | tf_op jit(solution)/shard_map/all_to_all | solution.py:132
  84.9 0.1 fusion.109
  85.0 10.1 %all-to-all-done.2 = bf16[32,2,16,128]{3,2,1,0:T(8,128)(2,1)S(1)} async-done(((bf16[32,2,16,128]{3,2,1,0:T(8,128)(2,1)}), bf16[32,2,16,128]{3,2,1,0:T(8,128)(2,1)S(1)}, u32[]{:S(2)}, u32[]{:S(2)}) %all-to-all-start.2) | async-done | bytes 262176 | tf_op jit(solution)/shard_map/all_to_all | solution.py:132
  95.1 0.3 fusion.108
  95.4 0.3 fusion.107
  95.8 0.3 convolution_subtract_fusion
  96.1 0.4 fusion.103
  96.6 0.4 fusion.137
  96.9 0.4 fusion.135
  97.3 0.4 fusion.14
  97.7 0.1 stack.37
  97.9 0.4 fusion.13
  98.2 0.1 stack.38
  98.4 0.7 maximum_multiply_fusion
  (63 shorter events, 1.3 us)
Async XLA Ops:
  1.3 19.4 %collective-permute-start = (bf16[2,128,512]{2,1,0:T(8,128)(2,1)S(1)}, bf16[2,128,512]{2,1,0:T(8,128)(2,1)S(1)}, u32[]{:S(2)}, u32[]{:S(2)}) collective-permute-start(bf16[2,128,512]{2,1,0:T(8,128)(2,1)S(1)} %get-tuple-element.19), channel_id=1, source_target_pairs={{0,1},{1,0},{2,3},{3,2},{4,5},{5,4},{6,7},{7,6},{8,9},{9,8},{10,11... | collective-permute-start | bytes 786440 | tf_op jit(solution)/shard_map/ppermute | solution.py:37
  4.4 24.2 %collective-permute-start.1 = (bf16[2,128,512]{2,1,0:T(8,128)(2,1)S(1)}, bf16[2,128,512]{2,1,0:T(8,128)(2,1)S(1)}, u32[]{:S(2)}, u32[]{:S(2)}) collective-permute-start(bf16[2,128,512]{2,1,0:T(8,128)(2,1)S(1)} %get-tuple-element.18), channel_id=1, source_target_pairs={{0,2},{1,3},{2,0},{3,1},{4,6},{5,7},{6,4},{7,5},{8,10},{9,11},{10,... | collective-permute-start | bytes 786440 | tf_op jit(solution)/shard_map/ppermute | solution.py:37
  7.0 21.6 %collective-permute-start.2 = (bf16[2,128,512]{2,1,0:T(8,128)(2,1)S(1)}, bf16[2,128,512]{2,1,0:T(8,128)(2,1)S(1)}, u32[]{:S(2)}, u32[]{:S(2)}) collective-permute-start(bf16[2,128,512]{2,1,0:T(8,128)(2,1)S(1)} %get-tuple-element.20), channel_id=1, source_target_pairs={{0,3},{1,2},{2,1},{3,0},{4,7},{5,6},{6,5},{7,4},{8,11},{9,10},{10,... | collective-permute-start | bytes 786440 | tf_op jit(solution)/shard_map/ppermute | solution.py:37
  9.8 31.4 %all-to-all-start = ((bf16[4,128,512]{2,1,0:T(8,128)(2,1)}), bf16[4,128,512]{2,1,0:T(8,128)(2,1)S(1)}, u32[]{:S(2)}, u32[]{:S(2)}) async-start(bf16[4,128,512]{2,1,0:T(8,128)(2,1)} %bitcast.12), calls=%async_computation | async-start | bytes 1048576 | tf_op jit(solution)/shard_map/all_to_all | solution.py:113
  17.1 3.2 %copy-start.2 = (bf16[2048,2048]{1,0:T(8,128)(2,1)}, bf16[2048,2048]{1,0:T(8,128)(2,1)S(1)}, u32[]{:S(2)}) copy-start(bf16[2048,2048]{1,0:T(8,128)(2,1)S(1)} %fusion.101) | copy-start | bytes 25165828
  20.7 7.9 %copy-start.3 = (bf16[2048,2048]{1,0:T(8,128)(2,1)}, bf16[2048,2048]{1,0:T(8,128)(2,1)S(1)}, u32[]{:S(2)}) copy-start(bf16[2048,2048]{1,0:T(8,128)(2,1)S(1)} %fusion.102) | copy-start | bytes 25165828
  30.2 6.2 %slice-start = ((s8[8388608]{0:T(1024)(128)(4,1)}), s8[4194304]{0:T(1024)(128)(4,1)S(1)}, s32[]{:S(2)}) async-start(s8[8388608]{0:T(1024)(128)(4,1)} %bitcast.103), calls=%async_computation.3 | async-start | bytes 8388608
  30.5 5.9 %slice-start.1 = ((s8[8388608]{0:T(1024)(128)(4,1)}), s8[4194304]{0:T(1024)(128)(4,1)S(1)}, s32[]{:S(2)}) async-start(s8[8388608]{0:T(1024)(128)(4,1)} %bitcast.103), calls=%async_computation.4 | async-start | bytes 8388608
  41.3 23.8 %all-to-all-start.1 = ((bf16[4,128,512]{2,1,0:T(8,128)(2,1)}), bf16[4,128,512]{2,1,0:T(8,128)(2,1)S(1)}, u32[]{:S(2)}, u32[]{:S(2)}) async-start(bf16[4,128,512]{2,1,0:T(8,128)(2,1)} %bitcast.94), calls=%async_computation.1 | async-start | bytes 1048576 | tf_op jit(solution)/shard_map/all_to_all | solution.py:113
  51.4 1.6 %copy-start = (f32[256,2048]{1,0:T(8,128)S(1)}, f32[256,2048]{1,0:T(8,128)}, u32[]{:S(2)}) copy-start(f32[256,2048]{1,0:T(8,128)} %fusion.293) | copy-start | bytes 6291460
  54.2 7.1 %slice-start.2 = ((s8[8388608]{0:T(1024)(128)(4,1)}), s8[4194304]{0:T(1024)(128)(4,1)S(1)}, s32[]{:S(2)}) async-start(s8[8388608]{0:T(1024)(128)(4,1)} %bitcast.105), calls=%async_computation.5 | async-start | bytes 8388608
  55.4 5.9 %slice-start.3 = ((s8[8388608]{0:T(1024)(128)(4,1)}), s8[4194304]{0:T(1024)(128)(4,1)S(1)}, s32[]{:S(2)}) async-start(s8[8388608]{0:T(1024)(128)(4,1)} %bitcast.105), calls=%async_computation.6 | async-start | bytes 8388608
  65.1 1.6 %copy-start.1 = (f32[256,2048]{1,0:T(8,128)S(1)}, f32[256,2048]{1,0:T(8,128)}, u32[]{:S(2)}) copy-start(f32[256,2048]{1,0:T(8,128)} %fusion.44) | copy-start | bytes 6291460
  78.8 16.3 %all-to-all-start.2 = ((bf16[32,2,16,128]{3,2,1,0:T(8,128)(2,1)}), bf16[32,2,16,128]{3,2,1,0:T(8,128)(2,1)S(1)}, u32[]{:S(2)}, u32[]{:S(2)}) async-start(bf16[32,2,16,128]{3,2,1,0:T(8,128)(2,1)} %copy.33), calls=%async_computation.2 | async-start | bytes 524288 | tf_op jit(solution)/shard_map/all_to_all | solution.py:132
